TPU v7x, 128 devices: a whole 4x4x4 slice. The times are simulated.
128 devices in a mesh: row: 8 (over y_lo, x), col: 16 (over y_hi, z, core).
Axes of the slice: x: 4, y: 4 (y_hi: 2, y_lo: 2; y = y_hi * 2 + y_lo), z: 4, core: 2. Of those that a mesh axis runs over, the one named last changes fastest.
Arguments:
- factor_panel: bfloat16 [12288, 98304], P('row', 'col'), may hold values from -1 to 1, as said below
- normals: bfloat16 [98304, 128], P(('col', 'row')), may hold values from -6 to 6
- bond_vectors: float32 [3, 4096, 12], P(None, ('col', 'row')), may hold values from -9 to 9
- neighbours: int32 [4096, 12], P(('col', 'row')), may hold values from 0 to 175
- send_atoms: int32 [128, 16], P(('col', 'row')), may hold values from 0 to 31
- radial_weight: bfloat16 [128, 128], replicated, may hold values from -1.5 to 1.5
- radial_bias: float32 [128], replicated, may hold values from -3 to 3
- middle_weight: bfloat16 [128, 128], replicated, may hold values from -0.5 to 0.5
- middle_bias: float32 [128], replicated, may hold values from -3 to 3
- output_weight: float32 [128], replicated, may hold values from -0.5 to 0.5
Outputs:
- atom_energy: float32 [4096, 128], P(('col', 'row'))
- forces: float32 [3, 4096, 128], P(None, ('col', 'row'))
Inputs may be any that keep to these rules, and one draw needn't show every extreme that they name: `factor_panel`: entries above the factor's diagonal are zero.
All inputs are finite; a program needn't handle non-finite values.
Results may differ from a plain program's by a relative error of at most 0.0052.
Values may be sent and summed in bfloat16 or wider, within the bound.
A program may use at most 128 MiB of HBM per device.

v0:
```python
import jax
import jax.numpy as jnp
from jax import lax
from jax.sharding import PartitionSpec as P

TILE = 16


def with_halo(cells, sides, width):
    for axis, dim in sides:
        count = lax.axis_size(axis)
        head = lax.slice_in_dim(cells, 0, width, axis=dim)
        tail = lax.slice_in_dim(cells, cells.shape[dim] - width, cells.shape[dim], axis=dim)
        cells = jnp.concatenate(
            [
                lax.ppermute(tail, axis, [(i, (i + 1) % count) for i in range(count)]),
                cells,
                lax.ppermute(head, axis, [((i + 1) % count, i) for i in range(count)]),
            ],
            axis=dim,
        )
    return cells


def pair_terms(
    own_disp,
    near_disp,
    bond_block,
    radial_weight,
    radial_bias,
    middle_weight,
    middle_bias,
    output_weight,
):
    vectors = bond_block[:, :, :, None] + near_disp - own_disp[:, :, None, :]
    squared = jnp.sum(vectors * vectors, axis=0)
    count = radial_weight.shape[0]
    centres = 30.0 * jnp.arange(count, dtype=jnp.float32) / (count - 1)
    spread = 90.0 / (count - 1)
    scaled = (squared[..., None] - centres) / spread
    basis = jnp.exp(-scaled * scaled)
    flat_basis = basis.reshape(-1, count)
    flat_scaled = scaled.reshape(-1, count)
    first = jnp.tanh(
        jnp.dot(flat_basis.astype(jnp.bfloat16), radial_weight, preferred_element_type=jnp.float32)
        + radial_bias
    )
    second = jnp.tanh(
        jnp.dot(first.astype(jnp.bfloat16), middle_weight, preferred_element_type=jnp.float32)
        + middle_bias
    )
    energies = jnp.sum(second * output_weight, axis=-1)
    back_second = ((1.0 - second * second) * output_weight).astype(jnp.bfloat16)
    back_first = (
        jnp.dot(back_second, middle_weight.T, preferred_element_type=jnp.float32)
        * (1.0 - first * first)
    ).astype(jnp.bfloat16)
    radial_grad = jnp.dot(back_first, radial_weight.T, preferred_element_type=jnp.float32)
    slopes = jnp.sum(radial_grad * flat_basis * (-2.0 / spread) * flat_scaled, axis=-1)
    shape = squared.shape
    atom_part = 0.5 * jnp.sum(energies.reshape(shape), axis=1)
    force_part = 2.0 * jnp.sum(slopes.reshape(shape)[None] * vectors, axis=2)
    return (atom_part, force_part)


def per_device(
    factor_panel,
    normals,
    bond_vectors,
    neighbours,
    send_atoms,
    radial_weight,
    radial_bias,
    middle_weight,
    middle_bias,
    output_weight,
):
    samples = normals.shape[1]
    local_rows = factor_panel.shape[0]
    partial_value = jnp.dot(
        factor_panel,
        lax.all_gather(normals, "row", axis=0, tiled=True),
        preferred_element_type=jnp.float32,
    )
    col_count = lax.axis_size("col")
    col_index = lax.axis_index("col")
    slab_rows = local_rows // col_count
    total = lax.psum(partial_value, "col")
    slab = lax.dynamic_slice_in_dim(total, col_index * slab_rows, slab_rows, 0)
    rows_count = lax.axis_size("row")
    row_index = lax.axis_index("row")
    tiles = slab_rows // TILE
    whole = lax.all_gather(slab, "row", axis=0, tiled=True)
    ordered = (
        whole.reshape(rows_count, tiles, TILE, samples)
        .transpose(1, 0, 2, 3)
        .reshape(rows_count * slab_rows, samples)
    )
    domain = lax.dynamic_slice_in_dim(ordered, row_index * slab_rows, slab_rows, 0)
    domain_atoms = bond_vectors.shape[1]
    neighbour_count = bond_vectors.shape[2]
    displacements = domain.reshape(3, domain_atoms, samples)
    sent = jnp.take(displacements, send_atoms[0], axis=1)
    beside_all = with_halo(sent[None, None], (("row", 0), ("col", 1)), 1)
    halo_atoms = jnp.moveaxis(beside_all, 2, 0).reshape(3, 9 * sent.shape[1], samples)
    pool = jnp.concatenate([displacements, halo_atoms], axis=1)
    nearby = jnp.take(pool, neighbours.reshape(-1), axis=1).reshape(
        3, domain_atoms, neighbour_count, samples
    )
    block_count = domain_atoms // 8
    own_blocks = displacements.reshape(3, block_count, 8, samples).transpose(1, 0, 2, 3)
    near_blocks = nearby.reshape(3, block_count, 8, neighbour_count, samples).transpose(
        1, 0, 2, 3, 4
    )
    bond_blocks = bond_vectors.reshape(3, block_count, 8, neighbour_count).transpose(1, 0, 2, 3)
    energy_blocks, force_blocks = lax.map(
        lambda items: pair_terms(
            items[0],
            items[1],
            items[2],
            radial_weight,
            radial_bias,
            middle_weight,
            middle_bias,
            output_weight,
        ),
        (own_blocks, near_blocks, bond_blocks),
    )
    atom_energy = energy_blocks.reshape(domain_atoms, samples)
    forces = force_blocks.transpose(1, 0, 2, 3).reshape(3, domain_atoms, samples)
    return (atom_energy, forces)


def solution(mesh):
    return jax.shard_map(
        per_device,
        mesh=mesh,
        in_specs=(
            P("row", "col"),
            P(("col", "row"), None),
            P(None, ("col", "row"), None),
            P(("col", "row"), None),
            P(("col", "row"), None),
            P(),
            P(),
            P(),
            P(),
            P(),
        ),
        out_specs=(P(("col", "row"), None), P(None, ("col", "row"), None)),
        check_vma=False,
    )
```

profile of v0, /device:TPU:103, one launch (start us, length us, event | category | flops | bytes accessed | tf_op | source)
XLA Modules:
  0.0 323.6 jit_solution(1270470169724800918)
XLA Ops:
  7.2 0.0 all-gather.2.cloned.1.call-start
  7.2 0.7 all-gather.2.cloned.1.call-update
  7.9 0.0 all-reduce.2.cloned.1.call-start
  8.0 35.4 %all-gather.2.cloned.1.call-done = bf16[6144,128]{1,0:T(8,128)(2,1)} async-done(((bf16[768,128]{1,0:T(8,128)(2,1)}), bf16[6144,128]{1,0:T(8,128)(2,1)}) %all-gather.2.cloned.1.call-update) | async-done | bytes 1572880 | tf_op jit(solution)/shard_map/all_gather | solution.py:82
  43.4 10.2 %fusion.22 = f32[1536,128]{1,0:T(8,128)} fusion(bf16[1536,6144]{1,0:T(8,128)(2,1)} %param.12, bf16[6144,128]{1,0:T(8,128)(2,1)} %all-gather.2.cloned.1.call-done), kind=kOutput, calls=%fused_computation.54 | convolution fusion | flops 2415919104 | bytes 21233664 | tf_op jit(solution)/shard_map/dot_general | solution.py:80
  53.6 0.0 all-reduce.2.cloned.1.call-update
  53.6 0.1 copy.31
  53.7 0.1 reshape.167
  53.9 147.7 %all-reduce.2.cloned.1.call-done = f32[1536,128]{1,0:T(8,128)} async-done(((f32[1536,128]{1,0:T(8,128)}), f32[1536,128]{1,0:T(8,128)}) %all-reduce.2.cloned.1.call-update) | async-done | bytes 786448 | tf_op jit(solution)/shard_map/psum | solution.py:88
  201.6 0.8 constant_dynamic-slice_fusion.1
  202.4 22.9 %all_gather.7 = f32[768,128]{1,0:T(8,128)S(1)} all-gather(f32[96,128]{1,0:T(8,128)S(1)} %constant_dynamic-slice_fusion.1), channel_id=1, replica_groups=mesh['row'=8,'col'=16] {'row'}, dimensions={0}, use_global_device_ids=true | all-gather | bytes 442368 | tf_op jit(solution)/shard_map/all_gather | solution.py:93
  225.4 0.6 gather_fusion
  226.0 0.1 bitcast_select_fusion
  226.1 0.9 collective-permute-start
  227.0 0.6 collective-permute-start.1
  227.7 0.1 copy.30
  227.8 1.2 collective-permute-done
  228.9 2.9 collective-permute-done.1
  231.9 9.4 %collective-permute-start.2 = (f32[3,1,3,16,128]{4,2,3,1,0:T(4,128)S(1)}, f32[3,1,3,16,128]{4,2,3,1,0:T(4,128)S(1)}, u32[]{:S(2)}, u32[]{:S(2)}) collective-permute-start(f32[3,1,3,16,128]{4,2,3,1,0:T(4,128)S(1)} %pad_maximum_fusion.2), channel_id=1, source_target_pairs={{0,1},{1,2},{2,3},{3,4},{4,5},{5,6},{6,7},{7,8},{8,9},{9,10},{10,1... | collective-permute-start | bytes 221192 | tf_op jit(solution)/shard_map/ppermute | solution.py:16
  241.3 1.6 collective-permute-done.2
  242.9 6.0 %collective-permute-done.3 = f32[3,1,3,16,128]{4,2,3,1,0:T(4,128)S(1)} collective-permute-done((f32[3,1,3,16,128]{4,2,3,1,0:T(4,128)S(1)}, f32[3,1,3,16,128]{4,2,3,1,0:T(4,128)S(1)}, u32[]{:S(2)}, u32[]{:S(2)}) %collective-permute-start.3) | collective-permute-done | bytes 73760 | tf_op jit(solution)/shard_map/ppermute | solution.py:18
  249.0 0.1 pad_maximum_fusion.1
  249.0 0.1 pad_maximum_fusion
  249.1 2.0 gather_fusion.1
  251.2 0.2 fusion.19
  251.4 64.7 %while.14 = (s32[]{:T(128)}, f32[4,8,128]{2,1,0:T(8,128)S(1)}, f32[4,3,8,128]{3,2,1,0:T(8,128)S(1)}, f32[4,3,8,12]{3,2,0,1:T(8,128)S(1)}, f32[4,3,8,12,128]{4,3,...) while((s32[]{:T(128)}, f32[4,8,128]{2,1,0:T(8,128)S(1)}, ...), condition=%wide.region_7.8_spmd, body=%wide.region_1.7_spmd.sunk | while | flops 1651777664 | bytes 57794740 | solution.py:116
  251.4 0.1 multiply_reduce_fusion.6
  251.6 2.5 fusion.42
  254.0 4.5 %multiply_reduce_fusion.7 = (f32[12288]{0:T(1024)S(1)}, f32[12288,128]{1,0:T(8,128)}) fusion(f32[128]{0:T(128)S(1)} %get-tuple-element.295, f32[128]{0:T(128)S(1)} %get-tuple-element.294, bf16[128,128]{1,0:T(8,128)(2,1)S(1)} %get-tuple-element.293, f32[12288,128]{1,0:T(8,128)S(1)} %fusion.42), kind=kOutput, calls=%fused_computation.15.clone.1 | convolution fusion | flops 408932352 | bytes 12665856 | tf_op jit(solution)/shard_map/while/body/eval_jaxpr/dot_general | solution.py:49
  258.6 8.7 %fusion.43 = f32[12288]{0:T(1024)S(1)} fusion(f32[128]{0:T(128)S(1)} %iota_multiply_fusion.2, f32[12288]{0:T(1024)S(1)} %sub.114, bf16[128,128]{1,0:T(8,128)(2,1)S(1)} %get-tuple-element.291, bf16[128,128]{1,0:T(8,128)(2,1)S(1)} %get-tuple-element.293, f32[12288,128]{1,0:T(8,128)} %copy-done, f32[12288,128]{1,0:T(8,128)} %get-tuple-element.258, ...), kind=kOutput, calls=%fused_computation.23.clone.1 | convolution fusion | flops 830459904 | bytes 12747776 | tf_op jit(solution)/shard_map/while/body/eval_jaxpr/dot_general | solution.py:58
  267.3 0.1 multiply_reduce_fusion.8
  267.6 0.1 multiply_reduce_fusion.6
  267.8 2.5 fusion.42
  270.2 4.5 %multiply_reduce_fusion.7 = (f32[12288]{0:T(1024)S(1)}, f32[12288,128]{1,0:T(8,128)}) fusion(f32[128]{0:T(128)S(1)} %get-tuple-element.295, f32[128]{0:T(128)S(1)} %get-tuple-element.294, bf16[128,128]{1,0:T(8,128)(2,1)S(1)} %get-tuple-element.293, f32[12288,128]{1,0:T(8,128)S(1)} %fusion.42), kind=kOutput, calls=%fused_computation.15.clone.1 | convolution fusion | flops 408932352 | bytes 12665856 | tf_op jit(solution)/shard_map/while/body/eval_jaxpr/dot_general | solution.py:49
  274.8 8.7 %fusion.43 = f32[12288]{0:T(1024)S(1)} fusion(f32[128]{0:T(128)S(1)} %iota_multiply_fusion.2, f32[12288]{0:T(1024)S(1)} %sub.114, bf16[128,128]{1,0:T(8,128)(2,1)S(1)} %get-tuple-element.291, bf16[128,128]{1,0:T(8,128)(2,1)S(1)} %get-tuple-element.293, f32[12288,128]{1,0:T(8,128)} %copy-done, f32[12288,128]{1,0:T(8,128)} %get-tuple-element.258, ...), kind=kOutput, calls=%fused_computation.23.clone.1 | convolution fusion | flops 830459904 | bytes 12747776 | tf_op jit(solution)/shard_map/while/body/eval_jaxpr/dot_general | solution.py:58
  283.5 0.1 multiply_reduce_fusion.8
  283.8 0.1 multiply_reduce_fusion.6
  283.9 2.5 fusion.42
  286.4 4.5 %multiply_reduce_fusion.7 = (f32[12288]{0:T(1024)S(1)}, f32[12288,128]{1,0:T(8,128)}) fusion(f32[128]{0:T(128)S(1)} %get-tuple-element.295, f32[128]{0:T(128)S(1)} %get-tuple-element.294, bf16[128,128]{1,0:T(8,128)(2,1)S(1)} %get-tuple-element.293, f32[12288,128]{1,0:T(8,128)S(1)} %fusion.42), kind=kOutput, calls=%fused_computation.15.clone.1 | convolution fusion | flops 408932352 | bytes 12665856 | tf_op jit(solution)/shard_map/while/body/eval_jaxpr/dot_general | solution.py:49
  290.9 8.7 %fusion.43 = f32[12288]{0:T(1024)S(1)} fusion(f32[128]{0:T(128)S(1)} %iota_multiply_fusion.2, f32[12288]{0:T(1024)S(1)} %sub.114, bf16[128,128]{1,0:T(8,128)(2,1)S(1)} %get-tuple-element.291, bf16[128,128]{1,0:T(8,128)(2,1)S(1)} %get-tuple-element.293, f32[12288,128]{1,0:T(8,128)} %copy-done, f32[12288,128]{1,0:T(8,128)} %get-tuple-element.258, ...), kind=kOutput, calls=%fused_computation.23.clone.1 | convolution fusion | flops 830459904 | bytes 12747776 | tf_op jit(solution)/shard_map/while/body/eval_jaxpr/dot_general | solution.py:58
  299.7 0.1 multiply_reduce_fusion.8
  300.0 0.1 multiply_reduce_fusion.6
  300.1 2.5 fusion.42
  302.6 4.5 %multiply_reduce_fusion.7 = (f32[12288]{0:T(1024)S(1)}, f32[12288,128]{1,0:T(8,128)}) fusion(f32[128]{0:T(128)S(1)} %get-tuple-element.295, f32[128]{0:T(128)S(1)} %get-tuple-element.294, bf16[128,128]{1,0:T(8,128)(2,1)S(1)} %get-tuple-element.293, f32[12288,128]{1,0:T(8,128)S(1)} %fusion.42), kind=kOutput, calls=%fused_computation.15.clone.1 | convolution fusion | flops 408932352 | bytes 12665856 | tf_op jit(solution)/shard_map/while/body/eval_jaxpr/dot_general | solution.py:49
  307.1 8.7 %fusion.43 = f32[12288]{0:T(1024)S(1)} fusion(f32[128]{0:T(128)S(1)} %iota_multiply_fusion.2, f32[12288]{0:T(1024)S(1)} %sub.114, bf16[128,128]{1,0:T(8,128)(2,1)S(1)} %get-tuple-element.291, bf16[128,128]{1,0:T(8,128)(2,1)S(1)} %get-tuple-element.293, f32[12288,128]{1,0:T(8,128)} %copy-done, f32[12288,128]{1,0:T(8,128)} %get-tuple-element.258, ...), kind=kOutput, calls=%fused_computation.23.clone.1 | convolution fusion | flops 830459904 | bytes 12747776 | tf_op jit(solution)/shard_map/while/body/eval_jaxpr/dot_general | solution.py:58
  315.9 0.1 multiply_reduce_fusion.8
  316.1 0.0 copy-start.7
  316.1 0.6 copy_bitcast_fusion
  (74 shorter events, 0.5 us)
Async XLA Ops:
  7.2 36.2 %all-gather.2.cloned.1.call-start = ((), (), s32[]{:S(2)}) async-start(), calls=%async_computation | async-start | bytes 1769472 | tf_op jit(solution)/shard_map/all_gather | solution.py:82
  7.9 45.7 %copy-start.5 = (s32[32,12]{0,1:T(8,128)S(1)}, s32[32,12]{0,1:T(8,128)}, u32[]{:S(2)}) copy-start(s32[32,12]{0,1:T(8,128)} %param.15) | copy-start | bytes 4612
  7.9 45.9 %copy-start.8 = (s32[1,16]{1,0:T(1,128)S(1)}, s32[1,16]{1,0:T(1,128)}, u32[]{:S(2)}) copy-start(s32[1,16]{1,0:T(1,128)} %param.16) | copy-start | bytes 196
  7.9 219.7 %copy-start.2 = (f32[3,32,12]{1,2,0:T(8,128)S(1)}, f32[3,32,12]{1,2,0:T(8,128)}, u32[]{:S(2)}) copy-start(f32[3,32,12]{1,2,0:T(8,128)} %param.14) | copy-start | bytes 13828
  7.9 193.6 %all-reduce.2.cloned.1.call-start = ((), (), s32[]{:S(2)}) async-start(), calls=%async_computation.1 | async-start | bytes 1572864 | tf_op jit(solution)/shard_map/psum | solution.py:88
  53.6 197.7 %copy-start.1 = (bf16[128,128]{1,0:T(8,128)(2,1)S(1)}, bf16[128,128]{1,0:T(8,128)(2,1)}, u32[]{:S(2)}) copy-start(bf16[128,128]{1,0:T(8,128)(2,1)} %param.19) | copy-start | bytes 98308
  53.6 197.8 %copy-start.3 = (f32[128]{0:T(128)S(1)}, f32[128]{0:T(128)}, u32[]{:S(2)}) copy-start(f32[128]{0:T(128)} %param.20) | copy-start | bytes 1540
  53.6 197.8 %copy-start.4 = (f32[128]{0:T(128)S(1)}, f32[128]{0:T(128)}, u32[]{:S(2)}) copy-start(f32[128]{0:T(128)} %param.21) | copy-start | bytes 1540
  53.6 197.8 %copy-start.6 = (bf16[128,128]{1,0:T(8,128)(2,1)S(1)}, bf16[128,128]{1,0:T(8,128)(2,1)}, u32[]{:S(2)}) copy-start(bf16[128,128]{1,0:T(8,128)(2,1)} %param.17) | copy-start | bytes 98308
  53.6 197.8 %copy-start.9 = (f32[128]{0:T(128)S(1)}, f32[128]{0:T(128)}, u32[]{:S(2)}) copy-start(f32[128]{0:T(128)} %param.18) | copy-start | bytes 1540
  226.1 2.8 collective-permute-start
  227.0 4.9 %collective-permute-start.1 = (f32[1,1,3,16,128]{4,2,3,1,0:T(4,128)S(1)}, f32[1,1,3,16,128]{4,2,3,1,0:T(4,128)S(1)}, u32[]{:S(2)}, u32[]{:S(2)}) collective-permute-start(f32[1,1,3,16,128]{4,2,3,1,0:T(4,128)S(1)} %bitcast_select_fusion), channel_id=1, source_target_pairs={{16,0},{32,16},{48,32},{64,48},{80,64},{96,80},{112,96},{0,112},{1... | collective-permute-start | bytes 73736 | tf_op jit(solution)/shard_map/ppermute | solution.py:18
  231.9 11.0 %collective-permute-start.2 = (f32[3,1,3,16,128]{4,2,3,1,0:T(4,128)S(1)}, f32[3,1,3,16,128]{4,2,3,1,0:T(4,128)S(1)}, u32[]{:S(2)}, u32[]{:S(2)}) collective-permute-start(f32[3,1,3,16,128]{4,2,3,1,0:T(4,128)S(1)} %pad_maximum_fusion.2), channel_id=1, source_target_pairs={{0,1},{1,2},{2,3},{3,4},{4,5},{5,6},{6,7},{7,8},{8,9},{9,10},{10,1... | collective-permute-start | bytes 221192 | tf_op jit(solution)/shard_map/ppermute | solution.py:16
  241.3 7.7 %collective-permute-start.3 = (f32[3,1,3,16,128]{4,2,3,1,0:T(4,128)S(1)}, f32[3,1,3,16,128]{4,2,3,1,0:T(4,128)S(1)}, u32[]{:S(2)}, u32[]{:S(2)}) collective-permute-start(f32[3,1,3,16,128]{4,2,3,1,0:T(4,128)S(1)} %pad_maximum_fusion.2), channel_id=1, source_target_pairs={{1,0},{2,1},{3,2},{4,3},{5,4},{6,5},{7,6},{8,7},{9,8},{10,9},{11,1... | collective-permute-start | bytes 221192 | tf_op jit(solution)/shard_map/ppermute | solution.py:18
  254.0 4.5 %copy-start = (f32[12288,128]{1,0:T(8,128)}, f32[12288,128]{1,0:T(8,128)S(1)}, u32[]{:S(2)}) copy-start(f32[12288,128]{1,0:T(8,128)S(1)} %fusion.42) | copy-start | bytes 18874372 | tf_op jit(solution)/shard_map/while
  270.2 4.5 %copy-start = (f32[12288,128]{1,0:T(8,128)}, f32[12288,128]{1,0:T(8,128)S(1)}, u32[]{:S(2)}) copy-start(f32[12288,128]{1,0:T(8,128)S(1)} %fusion.42) | copy-start | bytes 18874372 | tf_op jit(solution)/shard_map/while
  286.4 4.5 %copy-start = (f32[12288,128]{1,0:T(8,128)}, f32[12288,128]{1,0:T(8,128)S(1)}, u32[]{:S(2)}) copy-start(f32[12288,128]{1,0:T(8,128)S(1)} %fusion.42) | copy-start | bytes 18874372 | tf_op jit(solution)/shard_map/while
  302.6 4.5 %copy-start = (f32[12288,128]{1,0:T(8,128)}, f32[12288,128]{1,0:T(8,128)S(1)}, u32[]{:S(2)}) copy-start(f32[12288,128]{1,0:T(8,128)S(1)} %fusion.42) | copy-start | bytes 18874372 | tf_op jit(solution)/shard_map/while
  316.1 0.6 copy-start.7
Sparse Core Ops, SparseCore 0:
  9.6 33.7 all-gather.1
  53.8 147.7 all-reduce.1
where the time goes:
time: 324 us
  waiting for transfers between devices  196 us (60%)
  matrix products  73.1 us (23%)
  blocking collectives  22.9 us (7%)
  between operations  14.3 us (4%)
  starting transfers between devices  11 us (3%)
  local copies, waits for them, and re-layouts  4.61 us (1%)
    psum x1, waiting for transfers between devices, per_device(): total = lax.psum(partial_value, 'col')  148 us
    all_gather x1, waiting for transfers between devices, per_device(): lax.all_gather(normals, 'row', axis=0, tiled=True)  35.4 us
    dot_general x4, matrix products, pair_terms(): jnp.dot(back_first, radial_weight.T, preferred_element_type=jnp.float32)  35 us
    all_gather x1, blocking collectives, per_device(): whole = lax.all_gather(slab, 'row', axis=0, tiled=True)  22.9 us
    dot_general x4, matrix products, pair_terms(): jnp.dot(first.astype(jnp.bfloat16), middle_weight, preferred_element_type...  18.1 us
    ppermute x2, starting transfers between devices, with_halo(): lax.ppermute(tail, axis, [(i, (i + 1) % count) for i in range(count)])  10.3 us
    dot_general x1, matrix products, per_device(): jnp.dot(factor_panel, lax.all_gather(normals, 'row', axis=0, tiled=True),...  10.2 us
    dot_general x4, matrix products, pair_terms(): jnp.dot(flat_basis.astype(jnp.bfloat16), radial_weight, preferred_element...  9.83 us
  transfers between devices with their start and end apart: 6, of which 6 were waited for; matrix products, arithmetic and copies ran while one was open for 0% of the time, Pallas kernels for 0%

commit v1 on v0

--- a/solution.py
+++ b/solution.py
@@ -90,7 +90,9 @@
     rows_count = lax.axis_size("row")
     row_index = lax.axis_index("row")
     tiles = slab_rows // TILE
-    whole = lax.all_gather(slab, "row", axis=0, tiled=True)
+    whole = jnp.concatenate(
+        lax.all_to_all(jnp.stack([slab] * lax.axis_size("row")), "row", 0, 0), axis=0
+    )
     ordered = (
         whole.reshape(rows_count, tiles, TILE, samples)
         .transpose(1, 0, 2, 3)

time: 324 us -> 308 us (0.951)
  blocking collectives: 22.9 us -> 0 us
  waiting for transfers between devices: 196 us -> 201 us
    all_gather x1 -> x0, blocking collectives: 22.9 us -> none  [per_device(): whole = lax.all_gather(slab, 'row', axis=0, tiled=True)]
    all_to_all x0 -> x1, starting transfers between devices: none -> 5.16 us  [per_device(): lax.all_to_all(jnp.stack([slab] * lax.axis_size('row')), 'row', 0, 0)]
    all_to_all x0 -> x1, waiting for transfers between devices: none -> 4.57 us  [per_device(): lax.all_to_all(jnp.stack([slab] * lax.axis_size('row')), 'row', 0, 0)]
    ppermute x2, starting transfers between devices: 10.3 us -> 6.71 us  [with_halo(): lax.ppermute(tail, axis, [(i, (i + 1) % count) for i in range(count)])]
  transfers between devices with their start and end apart: 6 -> 7, of which waited for: 6 -> 7; matrix products, arithmetic and copies ran while one was open for 0% -> 0% of each run, Pallas kernels for 0% -> 0%
where the time goes in v1:
time: 308 us
  waiting for transfers between devices  201 us (65%)
  matrix products  73 us (24%)
  between operations  14.3 us (5%)
  starting transfers between devices  12 us (4%)
  local copies, waits for them, and re-layouts  5.39 us (2%)
    psum x1, waiting for transfers between devices, per_device(): total = lax.psum(partial_value, 'col')  148 us
    all_gather x1, waiting for transfers between devices, per_device(): lax.all_gather(normals, 'row', axis=0, tiled=True)  35.4 us
    dot_general x4, matrix products, pair_terms(): jnp.dot(back_first, radial_weight.T, preferred_element_type=jnp.float32)  35 us
    dot_general x4, matrix products, pair_terms(): jnp.dot(first.astype(jnp.bfloat16), middle_weight, preferred_element_type...  18 us
    dot_general x1, matrix products, per_device(): jnp.dot(factor_panel, lax.all_gather(normals, 'row', axis=0, tiled=True),...  10.2 us
    ppermute x2, waiting for transfers between devices, with_halo(): lax.ppermute(head, axis, [((i + 1) % count, i) for i in range(count)])  9.87 us
    dot_general x4, matrix products, pair_terms(): jnp.dot(flat_basis.astype(jnp.bfloat16), radial_weight, preferred_element...  9.82 us
    ppermute x2, starting transfers between devices, with_halo(): lax.ppermute(tail, axis, [(i, (i + 1) % count) for i in range(count)])  6.71 us
  transfers between devices with their start and end apart: 7, of which 7 were waited for; matrix products, arithmetic and copies ran while one was open for 0% of the time, Pallas kernels for 0%

profile of v1, /device:TPU:103, one launch (start us, length us, event | category | flops | bytes accessed | tf_op | source)
XLA Modules:
  0.0 307.8 jit_solution(4524308585044127769)
XLA Ops:
  7.2 0.0 all-gather.2.cloned.1.call-start
  7.2 0.7 all-gather.2.cloned.1.call-update
  7.9 0.0 all-reduce.2.cloned.1.call-start
  8.0 35.4 %all-gather.2.cloned.1.call-done = bf16[6144,128]{1,0:T(8,128)(2,1)} async-done(((bf16[768,128]{1,0:T(8,128)(2,1)}), bf16[6144,128]{1,0:T(8,128)(2,1)}) %all-gather.2.cloned.1.call-update) | async-done | bytes 1572880 | tf_op jit(solution)/shard_map/all_gather | solution.py:82
  43.4 10.2 %fusion.22 = f32[1536,128]{1,0:T(8,128)} fusion(bf16[1536,6144]{1,0:T(8,128)(2,1)} %param.12, bf16[6144,128]{1,0:T(8,128)(2,1)} %all-gather.2.cloned.1.call-done), kind=kOutput, calls=%fused_computation.54 | convolution fusion | flops 2415919104 | bytes 21233664 | tf_op jit(solution)/shard_map/dot_general | solution.py:80
  53.6 0.0 all-reduce.2.cloned.1.call-update
  53.7 147.9 %all-reduce.2.cloned.1.call-done = f32[1536,128]{1,0:T(8,128)} async-done(((f32[1536,128]{1,0:T(8,128)}), f32[1536,128]{1,0:T(8,128)}) %all-reduce.2.cloned.1.call-update) | async-done | bytes 786448 | tf_op jit(solution)/shard_map/psum | solution.py:88
  201.6 0.8 constant_dynamic-slice_fusion.1
  202.4 0.8 stack.2
  203.2 5.2 %all-to-all-start = ((f32[8,96,128]{2,1,0:T(8,128)}), f32[8,96,128]{2,1,0:T(8,128)S(1)}, u32[]{:S(2)}, u32[]{:S(2)}) async-start(f32[8,96,128]{2,1,0:T(8,128)} %stack.2), calls=%async_computation | async-start | bytes 786432 | tf_op jit(solution)/shard_map/all_to_all | solution.py:94
  208.4 0.1 copy.30
  208.4 0.1 reshape.165
  208.6 4.6 %all-to-all-done = f32[8,96,128]{2,1,0:T(8,128)S(1)} async-done(((f32[8,96,128]{2,1,0:T(8,128)}), f32[8,96,128]{2,1,0:T(8,128)S(1)}, u32[]{:S(2)}, u32[]{:S(2)}) %all-to-all-start) | async-done | bytes 393248 | tf_op jit(solution)/shard_map/all_to_all | solution.py:94
  213.2 0.6 gather_fusion
  213.8 0.1 bitcast_select_fusion
  213.9 2.1 collective-permute-start
  216.1 0.1 copy.29
  216.2 0.9 collective-permute-done
  217.0 3.9 %collective-permute-done.1 = f32[1,1,3,16,128]{4,2,3,1,0:T(4,128)S(1)} collective-permute-done((f32[1,1,3,16,128]{4,2,3,1,0:T(4,128)S(1)}, f32[1,1,3,16,128]{4,2,3,1,0:T(4,128)S(1)}, u32[]{:S(2)}, u32[]{:S(2)}) %collective-permute-start.1) | collective-permute-done | bytes 24608 | tf_op jit(solution)/shard_map/ppermute | solution.py:18
  220.9 4.6 %collective-permute-start.2 = (f32[3,1,3,16,128]{4,2,3,1,0:T(4,128)S(1)}, f32[3,1,3,16,128]{4,2,3,1,0:T(4,128)S(1)}, u32[]{:S(2)}, u32[]{:S(2)}) collective-permute-start(f32[3,1,3,16,128]{4,2,3,1,0:T(4,128)S(1)} %pad_maximum_fusion.2), channel_id=1, source_target_pairs={{0,1},{1,2},{2,3},{3,4},{4,5},{5,6},{6,7},{7,8},{8,9},{9,10},{10,1... | collective-permute-start | bytes 221192 | tf_op jit(solution)/shard_map/ppermute | solution.py:16
  225.6 1.6 collective-permute-done.2
  227.2 6.0 %collective-permute-done.3 = f32[3,1,3,16,128]{4,2,3,1,0:T(4,128)S(1)} collective-permute-done((f32[3,1,3,16,128]{4,2,3,1,0:T(4,128)S(1)}, f32[3,1,3,16,128]{4,2,3,1,0:T(4,128)S(1)}, u32[]{:S(2)}, u32[]{:S(2)}) %collective-permute-start.3) | collective-permute-done | bytes 73760 | tf_op jit(solution)/shard_map/ppermute | solution.py:18
  233.2 0.1 pad_maximum_fusion.1
  233.3 0.1 pad_maximum_fusion
  233.4 2.0 gather_fusion.1
  235.4 0.2 fusion.19
  235.6 64.7 %while.14 = (s32[]{:T(128)}, f32[4,8,128]{2,1,0:T(8,128)S(1)}, f32[4,3,8,128]{3,2,1,0:T(8,128)S(1)}, f32[4,3,8,12]{3,2,0,1:T(8,128)S(1)}, f32[4,3,8,12,128]{4,3,...) while((s32[]{:T(128)}, f32[4,8,128]{2,1,0:T(8,128)S(1)}, ...), condition=%wide.region_7.8_spmd, body=%wide.region_1.7_spmd.sunk | while | flops 1651777664 | bytes 57794740 | solution.py:118
  235.7 0.1 multiply_reduce_fusion.6
  235.8 2.5 fusion.42
  238.3 4.5 %multiply_reduce_fusion.7 = (f32[12288]{0:T(1024)S(1)}, f32[12288,128]{1,0:T(8,128)}) fusion(f32[128]{0:T(128)S(1)} %get-tuple-element.295, f32[128]{0:T(128)S(1)} %get-tuple-element.294, bf16[128,128]{1,0:T(8,128)(2,1)S(1)} %get-tuple-element.293, f32[12288,128]{1,0:T(8,128)S(1)} %fusion.42), kind=kOutput, calls=%fused_computation.15.clone.1 | convolution fusion | flops 408932352 | bytes 12665856 | tf_op jit(solution)/shard_map/while/body/eval_jaxpr/dot_general | solution.py:49
  242.8 8.7 %fusion.43 = f32[12288]{0:T(1024)S(1)} fusion(f32[128]{0:T(128)S(1)} %iota_multiply_fusion.2, f32[12288]{0:T(1024)S(1)} %sub.114, bf16[128,128]{1,0:T(8,128)(2,1)S(1)} %get-tuple-element.291, bf16[128,128]{1,0:T(8,128)(2,1)S(1)} %get-tuple-element.293, f32[12288,128]{1,0:T(8,128)} %copy-done, f32[12288,128]{1,0:T(8,128)} %get-tuple-element.258, ...), kind=kOutput, calls=%fused_computation.23.clone.1 | convolution fusion | flops 830459904 | bytes 12747776 | tf_op jit(solution)/shard_map/while/body/eval_jaxpr/dot_general | solution.py:58
  251.6 0.1 multiply_reduce_fusion.8
  251.8 0.1 multiply_reduce_fusion.6
  252.0 2.5 fusion.42
  254.5 4.5 %multiply_reduce_fusion.7 = (f32[12288]{0:T(1024)S(1)}, f32[12288,128]{1,0:T(8,128)}) fusion(f32[128]{0:T(128)S(1)} %get-tuple-element.295, f32[128]{0:T(128)S(1)} %get-tuple-element.294, bf16[128,128]{1,0:T(8,128)(2,1)S(1)} %get-tuple-element.293, f32[12288,128]{1,0:T(8,128)S(1)} %fusion.42), kind=kOutput, calls=%fused_computation.15.clone.1 | convolution fusion | flops 408932352 | bytes 12665856 | tf_op jit(solution)/shard_map/while/body/eval_jaxpr/dot_general | solution.py:49
  259.0 8.7 %fusion.43 = f32[12288]{0:T(1024)S(1)} fusion(f32[128]{0:T(128)S(1)} %iota_multiply_fusion.2, f32[12288]{0:T(1024)S(1)} %sub.114, bf16[128,128]{1,0:T(8,128)(2,1)S(1)} %get-tuple-element.291, bf16[128,128]{1,0:T(8,128)(2,1)S(1)} %get-tuple-element.293, f32[12288,128]{1,0:T(8,128)} %copy-done, f32[12288,128]{1,0:T(8,128)} %get-tuple-element.258, ...), kind=kOutput, calls=%fused_computation.23.clone.1 | convolution fusion | flops 830459904 | bytes 12747776 | tf_op jit(solution)/shard_map/while/body/eval_jaxpr/dot_general | solution.py:58
  267.7 0.1 multiply_reduce_fusion.8
  268.0 0.1 multiply_reduce_fusion.6
  268.2 2.5 fusion.42
  270.6 4.5 %multiply_reduce_fusion.7 = (f32[12288]{0:T(1024)S(1)}, f32[12288,128]{1,0:T(8,128)}) fusion(f32[128]{0:T(128)S(1)} %get-tuple-element.295, f32[128]{0:T(128)S(1)} %get-tuple-element.294, bf16[128,128]{1,0:T(8,128)(2,1)S(1)} %get-tuple-element.293, f32[12288,128]{1,0:T(8,128)S(1)} %fusion.42), kind=kOutput, calls=%fused_computation.15.clone.1 | convolution fusion | flops 408932352 | bytes 12665856 | tf_op jit(solution)/shard_map/while/body/eval_jaxpr/dot_general | solution.py:49
  275.1 8.7 %fusion.43 = f32[12288]{0:T(1024)S(1)} fusion(f32[128]{0:T(128)S(1)} %iota_multiply_fusion.2, f32[12288]{0:T(1024)S(1)} %sub.114, bf16[128,128]{1,0:T(8,128)(2,1)S(1)} %get-tuple-element.291, bf16[128,128]{1,0:T(8,128)(2,1)S(1)} %get-tuple-element.293, f32[12288,128]{1,0:T(8,128)} %copy-done, f32[12288,128]{1,0:T(8,128)} %get-tuple-element.258, ...), kind=kOutput, calls=%fused_computation.23.clone.1 | convolution fusion | flops 830459904 | bytes 12747776 | tf_op jit(solution)/shard_map/while/body/eval_jaxpr/dot_general | solution.py:58
  283.9 0.1 multiply_reduce_fusion.8
  284.2 0.1 multiply_reduce_fusion.6
  284.3 2.5 fusion.42
  286.8 4.5 %multiply_reduce_fusion.7 = (f32[12288]{0:T(1024)S(1)}, f32[12288,128]{1,0:T(8,128)}) fusion(f32[128]{0:T(128)S(1)} %get-tuple-element.295, f32[128]{0:T(128)S(1)} %get-tuple-element.294, bf16[128,128]{1,0:T(8,128)(2,1)S(1)} %get-tuple-element.293, f32[12288,128]{1,0:T(8,128)S(1)} %fusion.42), kind=kOutput, calls=%fused_computation.15.clone.1 | convolution fusion | flops 408932352 | bytes 12665856 | tf_op jit(solution)/shard_map/while/body/eval_jaxpr/dot_general | solution.py:49
  291.3 8.7 %fusion.43 = f32[12288]{0:T(1024)S(1)} fusion(f32[128]{0:T(128)S(1)} %iota_multiply_fusion.2, f32[12288]{0:T(1024)S(1)} %sub.114, bf16[128,128]{1,0:T(8,128)(2,1)S(1)} %get-tuple-element.291, bf16[128,128]{1,0:T(8,128)(2,1)S(1)} %get-tuple-element.293, f32[12288,128]{1,0:T(8,128)} %copy-done, f32[12288,128]{1,0:T(8,128)} %get-tuple-element.258, ...), kind=kOutput, calls=%fused_computation.23.clone.1 | convolution fusion | flops 830459904 | bytes 12747776 | tf_op jit(solution)/shard_map/while/body/eval_jaxpr/dot_general | solution.py:58
  300.1 0.1 multiply_reduce_fusion.8
  300.3 0.6 copy_bitcast_fusion
  (76 shorter events, 0.5 us)
Async XLA Ops:
  7.2 36.2 %all-gather.2.cloned.1.call-start = ((), (), s32[]{:S(2)}) async-start(), calls=%async_computation.1 | async-start | bytes 1769472 | tf_op jit(solution)/shard_map/all_gather | solution.py:82
  7.9 45.7 %copy-start.8 = (s32[1,16]{1,0:T(1,128)S(1)}, s32[1,16]{1,0:T(1,128)}, u32[]{:S(2)}) copy-start(s32[1,16]{1,0:T(1,128)} %param.16) | copy-start | bytes 196
  7.9 200.4 %copy-start.5 = (s32[32,12]{0,1:T(8,128)S(1)}, s32[32,12]{0,1:T(8,128)}, u32[]{:S(2)}) copy-start(s32[32,12]{0,1:T(8,128)} %param.15) | copy-start | bytes 4612
  7.9 208.1 %copy-start.2 = (f32[3,32,12]{1,2,0:T(8,128)S(1)}, f32[3,32,12]{1,2,0:T(8,128)}, u32[]{:S(2)}) copy-start(f32[3,32,12]{1,2,0:T(8,128)} %param.14) | copy-start | bytes 13828
  7.9 193.7 %all-reduce.2.cloned.1.call-start = ((), (), s32[]{:S(2)}) async-start(), calls=%async_computation.2 | async-start | bytes 1572864 | tf_op jit(solution)/shard_map/psum | solution.py:88
  53.6 182.0 %copy-start.1 = (bf16[128,128]{1,0:T(8,128)(2,1)S(1)}, bf16[128,128]{1,0:T(8,128)(2,1)}, u32[]{:S(2)}) copy-start(bf16[128,128]{1,0:T(8,128)(2,1)} %param.19) | copy-start | bytes 98308
  53.6 182.0 %copy-start.3 = (f32[128]{0:T(128)S(1)}, f32[128]{0:T(128)}, u32[]{:S(2)}) copy-start(f32[128]{0:T(128)} %param.20) | copy-start | bytes 1540
  53.6 182.0 %copy-start.4 = (f32[128]{0:T(128)S(1)}, f32[128]{0:T(128)}, u32[]{:S(2)}) copy-start(f32[128]{0:T(128)} %param.21) | copy-start | bytes 1540
  53.6 182.0 %copy-start.6 = (bf16[128,128]{1,0:T(8,128)(2,1)S(1)}, bf16[128,128]{1,0:T(8,128)(2,1)}, u32[]{:S(2)}) copy-start(bf16[128,128]{1,0:T(8,128)(2,1)} %param.17) | copy-start | bytes 98308
  53.6 182.0 %copy-start.9 = (f32[128]{0:T(128)S(1)}, f32[128]{0:T(128)}, u32[]{:S(2)}) copy-start(f32[128]{0:T(128)} %param.18) | copy-start | bytes 1540
  203.2 10.0 %all-to-all-start = ((f32[8,96,128]{2,1,0:T(8,128)}), f32[8,96,128]{2,1,0:T(8,128)S(1)}, u32[]{:S(2)}, u32[]{:S(2)}) async-start(f32[8,96,128]{2,1,0:T(8,128)} %stack.2), calls=%async_computation | async-start | bytes 786432 | tf_op jit(solution)/shard_map/all_to_all | solution.py:94
  213.9 3.1 %collective-permute-start = (f32[1,1,3,16,128]{4,2,3,1,0:T(4,128)S(1)}, f32[1,1,3,16,128]{4,2,3,1,0:T(4,128)S(1)}, u32[]{:S(2)}, u32[]{:S(2)}) collective-permute-start(f32[1,1,3,16,128]{4,2,3,1,0:T(4,128)S(1)} %bitcast_select_fusion), channel_id=1, source_target_pairs={{0,16},{16,32},{32,48},{48,64},{64,80},{80,96},{96,112},{112,0},{1... | collective-permute-start | bytes 73736 | tf_op jit(solution)/shard_map/ppermute | solution.py:16
  216.0 4.9 %collective-permute-start.1 = (f32[1,1,3,16,128]{4,2,3,1,0:T(4,128)S(1)}, f32[1,1,3,16,128]{4,2,3,1,0:T(4,128)S(1)}, u32[]{:S(2)}, u32[]{:S(2)}) collective-permute-start(f32[1,1,3,16,128]{4,2,3,1,0:T(4,128)S(1)} %bitcast_select_fusion), channel_id=1, source_target_pairs={{16,0},{32,16},{48,32},{64,48},{80,64},{96,80},{112,96},{0,112},{1... | collective-permute-start | bytes 73736 | tf_op jit(solution)/shard_map/ppermute | solution.py:18
  220.9 6.3 %collective-permute-start.2 = (f32[3,1,3,16,128]{4,2,3,1,0:T(4,128)S(1)}, f32[3,1,3,16,128]{4,2,3,1,0:T(4,128)S(1)}, u32[]{:S(2)}, u32[]{:S(2)}) collective-permute-start(f32[3,1,3,16,128]{4,2,3,1,0:T(4,128)S(1)} %pad_maximum_fusion.2), channel_id=1, source_target_pairs={{0,1},{1,2},{2,3},{3,4},{4,5},{5,6},{6,7},{7,8},{8,9},{9,10},{10,1... | collective-permute-start | bytes 221192 | tf_op jit(solution)/shard_map/ppermute | solution.py:16
  225.5 7.7 %collective-permute-start.3 = (f32[3,1,3,16,128]{4,2,3,1,0:T(4,128)S(1)}, f32[3,1,3,16,128]{4,2,3,1,0:T(4,128)S(1)}, u32[]{:S(2)}, u32[]{:S(2)}) collective-permute-start(f32[3,1,3,16,128]{4,2,3,1,0:T(4,128)S(1)} %pad_maximum_fusion.2), channel_id=1, source_target_pairs={{1,0},{2,1},{3,2},{4,3},{5,4},{6,5},{7,6},{8,7},{9,8},{10,9},{11,1... | collective-permute-start | bytes 221192 | tf_op jit(solution)/shard_map/ppermute | solution.py:18
  238.3 4.5 %copy-start = (f32[12288,128]{1,0:T(8,128)}, f32[12288,128]{1,0:T(8,128)S(1)}, u32[]{:S(2)}) copy-start(f32[12288,128]{1,0:T(8,128)S(1)} %fusion.42) | copy-start | bytes 18874372 | tf_op jit(solution)/shard_map/while
  254.4 4.5 %copy-start = (f32[12288,128]{1,0:T(8,128)}, f32[12288,128]{1,0:T(8,128)S(1)}, u32[]{:S(2)}) copy-start(f32[12288,128]{1,0:T(8,128)S(1)} %fusion.42) | copy-start | bytes 18874372 | tf_op jit(solution)/shard_map/while
  270.6 4.5 %copy-start = (f32[12288,128]{1,0:T(8,128)}, f32[12288,128]{1,0:T(8,128)S(1)}, u32[]{:S(2)}) copy-start(f32[12288,128]{1,0:T(8,128)S(1)} %fusion.42) | copy-start | bytes 18874372 | tf_op jit(solution)/shard_map/while
  286.8 4.5 %copy-start = (f32[12288,128]{1,0:T(8,128)}, f32[12288,128]{1,0:T(8,128)S(1)}, u32[]{:S(2)}) copy-start(f32[12288,128]{1,0:T(8,128)S(1)} %fusion.42) | copy-start | bytes 18874372 | tf_op jit(solution)/shard_map/while
  300.3 0.6 copy-start.7
Sparse Core Ops, SparseCore 0:
  9.6 33.7 all-gather.1
  53.8 147.7 all-reduce.1
